TPU v7x, 128 devices: a whole 4x4x4 slice. The times are simulated.
128 devices in a mesh: slab: 16 (over y, x), grp: 8 (over z, core).
Axes of the slice: x: 4, y: 4, z: 4, core: 2. Of those that a mesh axis runs over, the one named last changes fastest.
Arguments:
- initial: float32 [32, 64, 32, 256], P('grp', 'slab'), may hold values from 0 to 1
- target: float32 [32, 64, 32, 256], P('grp', 'slab'), may hold values from 0 to 0.6
- birth_step: int32 [64, 32, 256], P('slab'), may hold values from 0 to 4, as said below
- classes: int32 [32], P('grp'), may hold values from 0 to 3
- mobility: float32 [4, 4], replicated, may hold values from 0.2 to 2
Outputs:
- final_state: float32 [32, 64, 32, 256], P('grp', 'slab')
- initial_grad: float32 [32, 64, 32, 256], P('grp', 'slab')
- mobility_grad: float32 [4, 4], replicated
Inputs may be any that keep to these rules, and one draw needn't show every extreme that they name: A voxel takes part in step n when birth_step <= n; the value 4 means that it never takes part in the window; exactly one voxel has the value 0.
All inputs are finite; a program needn't handle non-finite values.
Results may differ from a plain program's by a relative error of at most 0.0001.
Values sent between devices are 32-bit elements; how exact they have to be, the bound alone decides.
No kernel may reach another device: no remote copies, remote signals or barrier semaphores. Data moves between devices by JAX's collectives and lax.ppermute only.
A program may use at most 64 MiB of HBM per device.

v0:
```python
import jax
import jax.numpy as jnp
from jax import lax
from jax.sharding import PartitionSpec as P

STEPS = 4
coupling = 0.3
stiffness = 1.0
time_step = 0.06


def extended_2(cells, sides, width):
    for axis, dim in sides:
        count = lax.axis_size(axis)
        ends = count - 1
        head = lax.slice_in_dim(cells, 0, width, axis=dim)
        tail = lax.slice_in_dim(cells, cells.shape[dim] - width, cells.shape[dim], axis=dim)
        cells = jnp.concatenate(
            [
                lax.ppermute(tail, axis, [(i, (i + 1) % count) for i in range(ends)]),
                cells,
                lax.ppermute(head, axis, [((i + 1) % count, i) for i in range(ends)]),
            ],
            axis=dim,
        )
    return cells


def laplace_local(extended):
    padded = jnp.pad(extended, ((0, 0), (0, 0), (1, 1), (1, 1)))
    centre = padded[:, 1:-1, 1:-1, 1:-1]
    return (
        padded[:, 2:, 1:-1, 1:-1]
        + padded[:, :-2, 1:-1, 1:-1]
        + padded[:, 1:-1, 2:, 1:-1]
        + padded[:, 1:-1, :-2, 1:-1]
        + padded[:, 1:-1, 1:-1, 2:]
        + padded[:, 1:-1, 1:-1, :-2]
        - 6.0 * centre
    )


def advance_local(fields, pair_rates, member, active):
    squared = fields * fields
    partial_sums = jnp.einsum("pk,pxzy->kxzy", member, squared, precision=lax.Precision.HIGHEST)
    class_sums = lax.psum(partial_sums, "grp")
    summed = jnp.sum(class_sums, axis=0)
    inverse = 1.0 / (1.0 + summed)
    driving = jnp.einsum("pk,kxzy->pxzy", pair_rates, class_sums, precision=lax.Precision.HIGHEST)
    rates = driving * inverse[None]
    extended = extended_2(fields, (("slab", 1),), 1)
    potential = (
        -fields
        + fields * squared
        + 2.0 * coupling * fields * (summed[None] - squared)
        - stiffness * laplace_local(extended)
    )
    weighted = active[None] * rates
    numerator, raw_denominator = lax.psum(
        (jnp.sum(weighted * potential, axis=(1, 2, 3)), jnp.sum(weighted, axis=(1, 2, 3))), "slab"
    )
    lagrange = numerator / jnp.maximum(raw_denominator, 1.0)
    updated = fields - time_step * weighted * (potential - lagrange[:, None, None, None])
    return (updated, potential, class_sums, numerator, raw_denominator)


def retreat(
    state_adj_next,
    fields,
    potential,
    class_sums,
    numerator,
    raw_denominator,
    member,
    pair_rates,
    active,
):
    squared = fields * fields
    summed = jnp.sum(class_sums, axis=0)
    inverse = 1.0 / (1.0 + summed)
    driving = jnp.einsum("pk,kxzy->pxzy", pair_rates, class_sums, precision=lax.Precision.HIGHEST)
    rates = driving * inverse[None]
    weighted = active[None] * rates
    denominator = jnp.maximum(raw_denominator, 1.0)
    lagrange = numerator / denominator
    scaled = time_step * active[None] * state_adj_next
    first_part = scaled * rates
    lagrange_adj = lax.psum(jnp.sum(first_part, axis=(1, 2, 3)), "slab")
    numer_adj = lagrange_adj / denominator
    potential_adj = weighted * numer_adj[:, None, None, None] - first_part
    extended = extended_2(potential_adj, (("slab", 1),), 1)
    curvature = laplace_local(extended)
    denom_adj = jnp.where(
        raw_denominator > 1.0, -lagrange_adj * numerator / (denominator * denominator), 0.0
    )
    rate_adj = -scaled * (potential - lagrange[:, None, None, None]) + active[None] * (
        numer_adj[:, None, None, None] * potential + denom_adj[:, None, None, None]
    )
    drive_adj = rate_adj * inverse[None]
    state_adj = (
        state_adj_next
        + potential_adj
        * (
            -1.0
            + 3.0 * squared
            + 2.0 * coupling * (summed[None] - squared)
            - 4.0 * coupling * squared
        )
        - stiffness * curvature
    )
    weighted_sums = jnp.einsum(
        "pk,pxzy->kxzy", pair_rates, drive_adj, precision=lax.Precision.HIGHEST
    )
    shared_sum = jnp.sum(
        2.0 * coupling * potential_adj * fields - (inverse * inverse)[None] * rate_adj * driving,
        axis=0,
    )
    weighted_sums, shared_sum = lax.psum((weighted_sums, shared_sum), "grp")
    class_adj = weighted_sums + shared_sum[None]
    state_adj = state_adj + 2.0 * fields * jnp.einsum(
        "pk,kxzy->pxzy", member, class_adj, precision=lax.Precision.HIGHEST
    )
    products = jnp.einsum("pxzy,kxzy->pk", drive_adj, class_sums, precision=lax.Precision.HIGHEST)
    mobility_term = jnp.dot(member.T, products, precision=lax.Precision.HIGHEST)
    return (state_adj, mobility_term)


def on_device(initial, target, birth_step, classes, mobility):
    classes_count = mobility.shape[0]
    member = (classes[:, None] == jnp.arange(classes_count, dtype=jnp.int32)[None, :]).astype(
        jnp.float32
    )
    pair_rates = jnp.dot(member, mobility, precision=lax.Precision.HIGHEST)
    fields = initial
    stored = []
    for step_index in range(STEPS):
        active = (birth_step <= step_index).astype(jnp.float32)
        updated, potential, class_sums, numerator, raw_denominator = advance_local(
            fields, pair_rates, member, active
        )
        stored.append((fields, potential, class_sums, numerator, raw_denominator, active))
        fields = updated
    state_adj = fields - target
    mobility_acc = jnp.zeros((classes_count, classes_count), jnp.float32)
    for step_index in range(STEPS - 1, -1, -1):
        saved_fields, potential, class_sums, numerator, raw_denominator, active = stored[step_index]
        state_adj, mobility_term = retreat(
            state_adj,
            saved_fields,
            potential,
            class_sums,
            numerator,
            raw_denominator,
            member,
            pair_rates,
            active,
        )
        mobility_acc = mobility_acc + mobility_term
    mobility_total = lax.psum(mobility_acc, ("slab", "grp"))
    scale = time_step * (initial.shape[1] * lax.axis_size("slab")) * initial.shape[2]
    return (fields, state_adj, mobility_total / scale)


def solution(mesh):
    return jax.shard_map(
        on_device,
        mesh=mesh,
        in_specs=(
            P("grp", "slab", None, None),
            P("grp", "slab", None, None),
            P("slab", None, None),
            P("grp"),
            P(),
        ),
        out_specs=(P("grp", "slab", None, None), P("grp", "slab", None, None), P()),
        check_vma=False,
    )
```

profile of v0, /device:TPU:0, one launch (start us, length us, event | category | flops | bytes accessed | tf_op | source)
XLA Modules:
  0.0 990.1 jit_solution(4415834130746513272)
XLA Ops:
  7.2 1.4 copy.20
  8.7 3.6 collective-permute-start.1
  13.7 1.8 fusion.9
  20.0 60.5 %all-reduce.25.cloned.1.call-done = f32[4,4,32,256]{3,0,2,1:T(4,128)} async-done(((f32[4,4,32,256]{3,0,2,1:T(4,128)}), f32[4,4,32,256]{3,0,2,1:T(4,128)}) %all-reduce.25.cloned.1.call-update) | async-done | bytes 524304 | tf_op jit(solution)/shard_map/psum | solution.py:46
  80.5 1.4 reduce_sum.196
  82.6 3.1 fusion.134
  85.7 40.3 %all-reduce.11 = (f32[4]{0:T(128)S(1)}, f32[4]{0:T(128)S(1)}) all-reduce(f32[4]{0:T(128)S(1)} %get-tuple-element.13, f32[4]{0:T(128)S(1)} %get-tuple-element.12), channel_id=1, replica_groups=mesh['slab'=16,'grp'=8] {'slab'}, use_global_device_ids=true, to_apply=%region_3.4 | all-reduce | flops 8 | bytes 64 | tf_op jit(solution)/shard_map/psum | solution.py:59
  126.6 1.7 multiply_subtract_fusion.11
  130.9 1.6 fusion.7
  132.6 3.9 collective-permute-done.2
  136.5 1.8 select_maximum_fusion.12
  138.2 52.1 %all-reduce.27.cloned.1.call-done = f32[4,4,32,256]{3,0,2,1:T(4,128)} async-done(((f32[4,4,32,256]{3,0,2,1:T(4,128)}), f32[4,4,32,256]{3,0,2,1:T(4,128)}) %all-reduce.27.cloned.1.call-update) | async-done | bytes 524304 | tf_op jit(solution)/shard_map/psum | solution.py:46
  190.3 1.4 reduce_sum.199
  192.4 4.1 fusion.135
  196.5 40.3 %all-reduce.10 = (f32[4]{0:T(128)S(1)}, f32[4]{0:T(128)S(1)}) all-reduce(f32[4]{0:T(128)S(1)} %get-tuple-element.11, f32[4]{0:T(128)S(1)} %get-tuple-element.10), channel_id=1, replica_groups=mesh['slab'=16,'grp'=8] {'slab'}, use_global_device_ids=true, to_apply=%region_9.10 | all-reduce | flops 8 | bytes 64 | tf_op jit(solution)/shard_map/psum | solution.py:59
  240.4 1.6 fusion.5
  242.2 3.7 collective-permute-done.4
  245.9 1.8 select_maximum_fusion.10
  247.7 52.0 %all-reduce.29.cloned.1.call-done = f32[4,4,32,256]{3,0,2,1:T(4,128)} async-done(((f32[4,4,32,256]{3,0,2,1:T(4,128)}), f32[4,4,32,256]{3,0,2,1:T(4,128)}) %all-reduce.29.cloned.1.call-update) | async-done | bytes 524304 | tf_op jit(solution)/shard_map/psum | solution.py:46
  299.7 1.4 reduce_sum.202
  301.8 4.6 fusion.136
  306.4 40.4 %all-reduce.9 = (f32[4]{0:T(128)S(1)}, f32[4]{0:T(128)S(1)}) all-reduce(f32[4]{0:T(128)} %get-tuple-element.9, f32[4]{0:T(128)} %get-tuple-element.8), channel_id=1, replica_groups=mesh['slab'=16,'grp'=8] {'slab'}, use_global_device_ids=true, to_apply=%region_15.16 | all-reduce | flops 8 | bytes 64 | tf_op jit(solution)/shard_map/psum | solution.py:59
  352.0 1.6 fusion.3
  353.7 4.0 collective-permute-done.6
  357.7 1.8 select_maximum_fusion.8
  359.5 51.8 %all-reduce.31.cloned.1.call-done = f32[4,4,32,256]{3,0,2,1:T(4,128)} async-done(((f32[4,4,32,256]{3,0,2,1:T(4,128)}), f32[4,4,32,256]{3,0,2,1:T(4,128)}) %all-reduce.31.cloned.1.call-update) | async-done | bytes 524304 | tf_op jit(solution)/shard_map/psum | solution.py:46
  411.3 1.4 reduce_sum.205
  413.4 5.4 fusion.137
  418.8 40.4 %all-reduce.8 = (f32[4]{0:T(128)S(1)}, f32[4]{0:T(128)S(1)}) all-reduce(f32[4]{0:T(128)} %get-tuple-element.7, f32[4]{0:T(128)} %get-tuple-element.6), channel_id=1, replica_groups=mesh['slab'=16,'grp'=8] {'slab'}, use_global_device_ids=true, to_apply=%region_21.22 | all-reduce | flops 8 | bytes 64 | tf_op jit(solution)/shard_map/psum | solution.py:59
  459.3 3.1 fusion.126
  462.4 35.5 %psum.187 = f32[4]{0:T(128)S(1)} all-reduce(f32[4]{0:T(128)S(1)} %get-tuple-element.48), channel_id=1, replica_groups=mesh['slab'=16,'grp'=8] {'slab'}, use_global_device_ids=true, to_apply=%region_25.26 | all-reduce | flops 4 | bytes 32 | tf_op jit(solution)/shard_map/psum | solution.py:88
  497.9 3.3 subtract_reduce_fusion.3
  501.9 4.5 collective-permute-start.9
  507.7 2.0 fusion.87
  511.0 3.6 convolution_bitcast_fusion.3
  515.5 2.7 select_maximum_fusion.6
  518.2 50.4 %all-reduce.39.cloned.1.call-done = (f32[4,4,32,256]{3,0,2,1:T(4,128)}, f32[4,32,256]{2,1,0:T(8,128)}) async-done(((f32[4,4,32,256]{3,0,2,1:T(4,128)}, f32[4,32,256]{2,1,0:T(8,128)}), (f32[4,4,32,256]{3,0,2,1:T(4,128)}, f32[4,32,256]{2,1,0:T(8,128)})) %all-reduce.39.cloned.1.call-update) | async-done | bytes 655376 | tf_op jit(solution)/shard_map/psum | solution.py:118
  568.6 6.0 fusion.127
  574.6 40.4 %psum.190 = f32[4]{0:T(128)S(1)} all-reduce(f32[4]{0:T(128)} %get-tuple-element.99), channel_id=1, replica_groups=mesh['slab'=16,'grp'=8] {'slab'}, use_global_device_ids=true, to_apply=%region_30.31 | all-reduce | flops 4 | bytes 32 | tf_op jit(solution)/shard_map/psum | solution.py:88
  615.7 3.0 subtract_reduce_fusion.2
  619.5 1.9 collective-permute-start.11
  622.7 2.0 fusion.84
  624.8 2.5 convolution_bitcast_fusion.2
  627.3 1.6 convolution_add_fusion.2
  628.9 2.7 select_maximum_fusion.4
  631.7 51.4 %all-reduce.37.cloned.1.call-done = (f32[4,4,32,256]{3,0,2,1:T(4,128)}, f32[4,32,256]{2,1,0:T(8,128)}) async-done(((f32[4,4,32,256]{3,0,2,1:T(4,128)}, f32[4,32,256]{2,1,0:T(8,128)}), (f32[4,4,32,256]{3,0,2,1:T(4,128)}, f32[4,32,256]{2,1,0:T(8,128)})) %all-reduce.37.cloned.1.call-update) | async-done | bytes 655376 | tf_op jit(solution)/shard_map/psum | solution.py:118
  683.1 5.8 fusion.128
  688.9 40.8 %psum.193 = f32[4]{0:T(128)S(1)} all-reduce(f32[4]{0:T(128)} %get-tuple-element.101), channel_id=1, replica_groups=mesh['slab'=16,'grp'=8] {'slab'}, use_global_device_ids=true, to_apply=%region_35.36 | all-reduce | flops 4 | bytes 32 | tf_op jit(solution)/shard_map/psum | solution.py:88
  730.3 2.9 subtract_reduce_fusion.1
  733.2 1.4 collective-permute-start.13
  736.0 2.0 fusion.81
  738.1 2.5 convolution_bitcast_fusion.1
  740.6 1.6 convolution_add_fusion.1
  742.2 1.8 select_maximum_fusion.2
  744.0 52.3 %all-reduce.35.cloned.1.call-done = (f32[4,4,32,256]{3,0,2,1:T(4,128)}, f32[4,32,256]{2,1,0:T(8,128)}) async-done(((f32[4,4,32,256]{3,0,2,1:T(4,128)}, f32[4,32,256]{2,1,0:T(8,128)}), (f32[4,4,32,256]{3,0,2,1:T(4,128)}, f32[4,32,256]{2,1,0:T(8,128)})) %all-reduce.35.cloned.1.call-update) | async-done | bytes 655376 | tf_op jit(solution)/shard_map/psum | solution.py:118
  796.3 5.8 fusion.129
  802.1 40.4 %psum.196 = f32[4]{0:T(128)S(1)} all-reduce(f32[4]{0:T(128)} %get-tuple-element.103), channel_id=1, replica_groups=mesh['slab'=16,'grp'=8] {'slab'}, use_global_device_ids=true, to_apply=%region_40.41 | all-reduce | flops 4 | bytes 32 | tf_op jit(solution)/shard_map/psum | solution.py:88
  843.3 3.0 subtract_reduce_fusion
  846.3 2.5 convolution_bitcast_fusion
  849.1 2.0 fusion.78
  851.1 62.5 %psum.199 = f32[4,4]{1,0:T(4,128)S(1)} all-reduce(f32[4,4]{1,0:T(4,128)S(1)} %convolution_add_fusion), channel_id=1, replica_groups=mesh['slab'=16,'grp'=8] {'slab','grp'}, use_global_device_ids=true, to_apply=%region_44.45 | all-reduce | flops 16 | bytes 128 | tf_op jit(solution)/shard_map/psum | solution.py:159
  917.6 4.4 collective-permute-done.14
  922.6 56.6 %all-reduce.33.cloned.1.call-done = (f32[4,4,32,256]{3,0,2,1:T(4,128)}, f32[4,32,256]{2,1,0:T(8,128)}) async-done(((f32[4,4,32,256]{3,0,2,1:T(4,128)}, f32[4,32,256]{2,1,0:T(8,128)}), (f32[4,4,32,256]{3,0,2,1:T(4,128)}, f32[4,32,256]{2,1,0:T(8,128)})) %all-reduce.33.cloned.1.call-update) | async-done | bytes 655376 | tf_op jit(solution)/shard_map/psum | solution.py:118
  979.2 3.0 fusion.20
  (177 shorter events, 36.1 us)
Async XLA Ops:
  7.2 12.0 %copy-start = (f32[4,4]{1,0:T(4,128)S(1)}, f32[4,4]{1,0:T(4,128)}, u32[]{:S(2)}) copy-start(f32[4,4]{1,0:T(4,128)} %param.9) | copy-start | bytes 196
  7.2 6.5 copy-start.1
  7.2 6.5 copy-start.40
  7.2 73.3 %all-reduce.25.cloned.1.call-start = ((), (), s32[]{:S(2)}) async-start(), calls=%async_computation | async-start | bytes 1048576 | tf_op jit(solution)/shard_map/psum | solution.py:46
  8.7 6.9 copy-start.39
  8.7 10.6 %collective-permute-start.1 = (f32[4,1,32,256]{3,0,2,1:T(4,128)S(1)}, f32[4,1,32,256]{3,0,2,1:T(4,128)S(1)}, u32[]{:S(2)}, u32[]{:S(2)}) collective-permute-start(f32[4,1,32,256]{3,0,2,1:T(4,128)S(1)} %get-tuple-element.71), channel_id=1, source_target_pairs={{0,8},{8,16},{16,24},{24,32},{32,40},{40,48},{48,56},{56,64},{64,7... | collective-permute-start | bytes 393224 | tf_op jit(solution)/shard_map/ppermute | solution.py:20
  12.4 7.0 collective-permute-start
  15.5 174.8 %all-reduce.27.cloned.1.call-start = ((), (), s32[]{:S(2)}) async-start(), calls=%async_computation.1 | async-start | bytes 1048576 | tf_op jit(solution)/shard_map/psum | solution.py:46
  19.3 61.2 %copy-start.35 = (f32[4,1,32,256]{3,0,2,1:T(4,128)}, f32[4,1,32,256]{3,0,2,1:T(4,128)S(1)}, u32[]{:S(2)}) copy-start(f32[4,1,32,256]{3,0,2,1:T(4,128)S(1)} %collective-permute-done.1) | copy-start | bytes 393220
  85.7 42.6 %copy-start.5 = (f32[4,4,32,256]{3,0,2,1:T(4,128)}, f32[4,4,32,256]{3,0,2,1:T(4,128)S(1)}, u32[]{:S(2)}) copy-start(f32[4,4,32,256]{3,0,2,1:T(4,128)S(1)} %get-tuple-element.56) | copy-start | bytes 1572868
  85.7 42.6 %copy-start.7 = (f32[4,4,32,256]{3,0,2,1:T(4,128)}, f32[4,4,32,256]{3,0,2,1:T(4,128)S(1)}, u32[]{:S(2)}) copy-start(f32[4,4,32,256]{3,0,2,1:T(4,128)S(1)} %get-tuple-element.95) | copy-start | bytes 1572868
  128.3 4.3 collective-permute-start.3
  129.6 6.9 collective-permute-start.2
  132.5 59.8 %copy-start.21 = (f32[4,32,256]{2,1,0:T(8,128)S(1)}, f32[4,32,256]{2,1,0:T(8,128)}, u32[]{:S(2)}) copy-start(f32[4,32,256]{2,1,0:T(8,128)} %convert_element_type.23) | copy-start | bytes 393220
  132.6 167.1 %all-reduce.29.cloned.1.call-start = ((), (), s32[]{:S(2)}) async-start(), calls=%async_computation.2 | async-start | bytes 1048576 | tf_op jit(solution)/shard_map/psum | solution.py:46
  191.7 4.8 copy-start.30
  196.5 41.3 %copy-start.10 = (f32[4,4,32,256]{3,0,2,1:T(4,128)}, f32[4,4,32,256]{3,0,2,1:T(4,128)S(1)}, u32[]{:S(2)}) copy-start(f32[4,4,32,256]{3,0,2,1:T(4,128)S(1)} %get-tuple-element.55) | copy-start | bytes 1572868
  196.5 41.3 %copy-start.12 = (f32[4,4,32,256]{3,0,2,1:T(4,128)}, f32[4,4,32,256]{3,0,2,1:T(4,128)S(1)}, u32[]{:S(2)}) copy-start(f32[4,4,32,256]{3,0,2,1:T(4,128)S(1)} %get-tuple-element.96) | copy-start | bytes 1572868
  237.8 4.5 collective-permute-start.5
  239.1 6.9 collective-permute-start.4
  242.0 59.8 %copy-start.22 = (f32[4,32,256]{2,1,0:T(8,128)S(1)}, f32[4,32,256]{2,1,0:T(8,128)}, u32[]{:S(2)}) copy-start(f32[4,32,256]{2,1,0:T(8,128)} %convert_element_type.24) | copy-start | bytes 393220
  242.0 169.3 %all-reduce.31.cloned.1.call-start = ((), (), s32[]{:S(2)}) async-start(), calls=%async_computation.3 | async-start | bytes 1048576 | tf_op jit(solution)/shard_map/psum | solution.py:46
  301.0 5.3 copy-start.32
  306.4 43.0 %copy-start.15 = (f32[4,4,32,256]{3,0,2,1:T(4,128)}, f32[4,4,32,256]{3,0,2,1:T(4,128)S(1)}, u32[]{:S(2)}) copy-start(f32[4,4,32,256]{3,0,2,1:T(4,128)S(1)} %get-tuple-element.54) | copy-start | bytes 1572868
  306.4 43.0 %copy-start.17 = (f32[4,4,32,256]{3,0,2,1:T(4,128)}, f32[4,4,32,256]{3,0,2,1:T(4,128)S(1)}, u32[]{:S(2)}) copy-start(f32[4,4,32,256]{3,0,2,1:T(4,128)S(1)} %get-tuple-element.97) | copy-start | bytes 1572868
  349.4 4.3 collective-permute-start.7
  350.7 7.1 collective-permute-start.6
  353.6 59.7 %copy-start.23 = (f32[4,32,256]{2,1,0:T(8,128)S(1)}, f32[4,32,256]{2,1,0:T(8,128)}, u32[]{:S(2)}) copy-start(f32[4,32,256]{2,1,0:T(8,128)} %convert_element_type.25) | copy-start | bytes 393220
  353.6 215.0 %all-reduce.39.cloned.1.call-start = ((), (), s32[]{:S(2)}) async-start(), calls=%async_computation.7 | async-start | bytes 1310720 | tf_op jit(solution)/shard_map/psum | solution.py:118
  353.7 57.6 %copy-start.37 = (f32[4,1,32,256]{3,0,2,1:T(4,128)}, f32[4,1,32,256]{3,0,2,1:T(4,128)S(1)}, u32[]{:S(2)}) copy-start(f32[4,1,32,256]{3,0,2,1:T(4,128)S(1)} %collective-permute-done.7) | copy-start | bytes 393220
  357.7 54.9 %copy-start.38 = (f32[4,1,32,256]{3,0,2,1:T(4,128)}, f32[4,1,32,256]{3,0,2,1:T(4,128)S(1)}, u32[]{:S(2)}) copy-start(f32[4,1,32,256]{3,0,2,1:T(4,128)S(1)} %collective-permute-done.6) | copy-start | bytes 393220
  412.7 6.1 copy-start.33
  413.4 45.9 %copy-start.2 = (f32[4,32,256]{2,1,0:T(8,128)}, f32[4,32,256]{2,1,0:T(8,128)S(1)}, u32[]{:S(2)}) copy-start(f32[4,32,256]{2,1,0:T(8,128)S(1)} %get-tuple-element.80) | copy-start | bytes 393220
  413.4 45.9 %copy-start.24 = (f32[4,32,256]{2,1,0:T(8,128)S(1)}, f32[4,32,256]{2,1,0:T(8,128)}, u32[]{:S(2)}) copy-start(f32[4,32,256]{2,1,0:T(8,128)} %get-tuple-element.51) | copy-start | bytes 393220
  418.8 43.6 %copy-start.19 = (f32[4,4,32,256]{3,0,2,1:T(4,128)}, f32[4,4,32,256]{3,0,2,1:T(4,128)S(1)}, u32[]{:S(2)}) copy-start(f32[4,4,32,256]{3,0,2,1:T(4,128)S(1)} %get-tuple-element.53) | copy-start | bytes 1572868
  459.2 3.1 copy-start.43
  497.9 9.8 copy-start.3
  501.2 8.6 copy-start.18
  501.9 13.6 %collective-permute-start.9 = (f32[4,1,32,256]{3,0,2,1:T(4,128)}, f32[4,1,32,256]{3,0,2,1:T(4,128)}, u32[]{:S(2)}, u32[]{:S(2)}) collective-permute-start(f32[4,1,32,256]{3,0,2,1:T(4,128)} %get-tuple-element.63), channel_id=1, source_target_pairs={{0,8},{8,16},{16,24},{24,32},{32,40},{40,48},{48,56},{56,64},{64,7... | collective-permute-start | bytes 393224 | tf_op jit(solution)/shard_map/ppermute | solution.py:20
  506.4 9.0 collective-permute-start.8
  510.7 172.4 %all-reduce.37.cloned.1.call-start = ((), (), s32[]{:S(2)}) async-start(), calls=%async_computation.6 | async-start | bytes 1310720 | tf_op jit(solution)/shard_map/psum | solution.py:118
  568.6 47.1 %copy-start.16 = (f32[4,4,32,256]{3,0,2,1:T(4,128)S(1)}, f32[4,4,32,256]{3,0,2,1:T(4,128)}, u32[]{:S(2)}) copy-start(f32[4,4,32,256]{3,0,2,1:T(4,128)} %copy-done.15) | copy-start | bytes 1572868
  618.7 6.1 copy-start.14
  619.5 9.5 collective-permute-start.11
  621.4 7.5 collective-permute-start.10
  624.8 171.5 %all-reduce.35.cloned.1.call-start = ((), (), s32[]{:S(2)}) async-start(), calls=%async_computation.5 | async-start | bytes 1310720 | tf_op jit(solution)/shard_map/psum | solution.py:118
  627.3 55.8 %copy-start.13 = (f32[4,4,32,256]{3,0,2,1:T(4,128)S(1)}, f32[4,4,32,256]{3,0,2,1:T(4,128)}, u32[]{:S(2)}) copy-start(f32[4,4,32,256]{3,0,2,1:T(4,128)} %copy-done.12) | copy-start | bytes 1572868
  627.3 55.8 %copy-start.29 = (f32[4,32,256]{2,1,0:T(8,128)S(1)}, f32[4,32,256]{2,1,0:T(8,128)}, u32[]{:S(2)}) copy-start(f32[4,32,256]{2,1,0:T(8,128)} %get-tuple-element.81) | copy-start | bytes 393220
  683.1 47.2 %copy-start.11 = (f32[4,4,32,256]{3,0,2,1:T(4,128)S(1)}, f32[4,4,32,256]{3,0,2,1:T(4,128)}, u32[]{:S(2)}) copy-start(f32[4,4,32,256]{3,0,2,1:T(4,128)} %copy-done.10) | copy-start | bytes 1572868
  733.2 4.9 copy-start.9
  733.2 9.0 collective-permute-start.13
  734.7 7.6 collective-permute-start.12
  738.0 241.2 %all-reduce.33.cloned.1.call-start = ((), (), s32[]{:S(2)}) async-start(), calls=%async_computation.4 | async-start | bytes 1310720 | tf_op jit(solution)/shard_map/psum | solution.py:118
  740.6 55.7 %copy-start.8 = (f32[4,4,32,256]{3,0,2,1:T(4,128)S(1)}, f32[4,4,32,256]{3,0,2,1:T(4,128)}, u32[]{:S(2)}) copy-start(f32[4,4,32,256]{3,0,2,1:T(4,128)} %copy-done.7) | copy-start | bytes 1572868
  740.6 55.7 %copy-start.28 = (f32[4,32,256]{2,1,0:T(8,128)S(1)}, f32[4,32,256]{2,1,0:T(8,128)}, u32[]{:S(2)}) copy-start(f32[4,32,256]{2,1,0:T(8,128)} %get-tuple-element.83) | copy-start | bytes 393220
  740.6 55.7 %copy-start.31 = (f32[4,32,256]{2,1,0:T(8,128)S(1)}, f32[4,32,256]{2,1,0:T(8,128)}, u32[]{:S(2)}) copy-start(f32[4,32,256]{2,1,0:T(8,128)} %copy-done.30) | copy-start | bytes 393220
  796.3 46.9 %copy-start.6 = (f32[4,4,32,256]{3,0,2,1:T(4,128)S(1)}, f32[4,4,32,256]{3,0,2,1:T(4,128)}, u32[]{:S(2)}) copy-start(f32[4,4,32,256]{3,0,2,1:T(4,128)} %copy-done.5) | copy-start | bytes 1572868
  796.3 46.9 %copy-start.20 = (f32[4,32,256]{2,1,0:T(8,128)S(1)}, f32[4,32,256]{2,1,0:T(8,128)}, u32[]{:S(2)}) copy-start(f32[4,32,256]{2,1,0:T(8,128)} %convert_element_type.22) | copy-start | bytes 393220
  796.3 46.9 %copy-start.25 = (f32[4,32,256]{2,1,0:T(8,128)S(1)}, f32[4,32,256]{2,1,0:T(8,128)}, u32[]{:S(2)}) copy-start(f32[4,32,256]{2,1,0:T(8,128)} %get-tuple-element.73) | copy-start | bytes 393220
  843.3 5.6 copy-start.50
  913.7 3.9 collective-permute-start.15
  915.0 7.0 collective-permute-start.14
  916.3 62.9 %copy-start.27 = (f32[4,32,256]{2,1,0:T(8,128)S(1)}, f32[4,32,256]{2,1,0:T(8,128)}, u32[]{:S(2)}) copy-start(f32[4,32,256]{2,1,0:T(8,128)} %copy-done.26) | copy-start | bytes 393220
  916.3 62.9 %copy-start.34 = (f32[4,4,32,256]{3,0,2,1:T(4,128)S(1)}, f32[4,4,32,256]{3,0,2,1:T(4,128)}, u32[]{:S(2)}) copy-start(f32[4,4,32,256]{3,0,2,1:T(4,128)} %get-tuple-element.104) | copy-start | bytes 1572868
  (11 other events, 10.8 us)
Sparse Core Ops, SparseCore 0:
  15.7 64.7 all-reduce.24
  132.7 57.5 all-reduce.26
  242.1 57.5 all-reduce.28
  353.7 57.5 all-reduce.30
  510.8 57.7 all-reduce.38
  624.9 58.1 all-reduce.36
  738.1 58.1 all-reduce.34
  916.5 62.6 all-reduce.32
where the time goes:
time: 999 us; the launch traced here: 990 us
  waiting for transfers between devices  444 us (44%)
  blocking collectives  381 us (38%)
  matrix products  68.3 us (7%)
  other arithmetic  46.8 us (5%)
  starting transfers between devices  27.8 us (3%)
  between operations  15 us (2%)
    psum x4, waiting for transfers between devices, advance_local(): class_sums = lax.psum(partial_sums, 'grp')  216 us
    psum x4, waiting for transfers between devices, retreat(): weighted_sums, shared_sum = lax.psum((weighted_sums, shared_sum), 'grp')  211 us
    psum x4, blocking collectives, advance_local(): lax.psum((jnp.sum(weighted * potential, axis=(1, 2, 3)), jnp.sum(weighted...  162 us
    psum x4, blocking collectives, retreat(): lagrange_adj = lax.psum(jnp.sum(first_part, axis=(1, 2, 3)), 'slab')  157 us
    psum x1, blocking collectives, on_device(): mobility_total = lax.psum(mobility_acc, ('slab', 'grp'))  62.5 us
    dot_general x4, matrix products, retreat(): jnp.einsum('pk,kxzy->pxzy', member, class_adj, precision=lax.Precision.HI...  20.6 us
  transfers between devices with their start and end apart: 24, of which 13 were waited for; matrix products, arithmetic and copies ran while one was open for 4% of the time, Pallas kernels for 0%

commit v1 on v0

--- a/solution.py
+++ b/solution.py
@@ -1,12 +1,21 @@
+import functools
 import jax
 import jax.numpy as jnp
 from jax import lax
 from jax.sharding import PartitionSpec as P
+from jax.lax import all_gather
 
 STEPS = 4
 coupling = 0.3
 stiffness = 1.0
 time_step = 0.06
+
+
+def view_the_array(slab_in, ax_name):
+    return all_gather(slab_in, ax_name).sum(axis=0)
+
+
+settle_series_all = functools.partial(view_the_array, ax_name="grp")
 
 
 def extended_2(cells, sides, width):
@@ -43,7 +52,7 @@
 def advance_local(fields, pair_rates, member, active):
     squared = fields * fields
     partial_sums = jnp.einsum("pk,pxzy->kxzy", member, squared, precision=lax.Precision.HIGHEST)
-    class_sums = lax.psum(partial_sums, "grp")
+    class_sums = settle_series_all(partial_sums)
     summed = jnp.sum(class_sums, axis=0)
     inverse = 1.0 / (1.0 + summed)
     driving = jnp.einsum("pk,kxzy->pxzy", pair_rates, class_sums, precision=lax.Precision.HIGHEST)

time: 999 us -> 886 us (0.89)
  waiting for transfers between devices: 444 us -> 323 us
  other arithmetic: 46.8 us -> 59.7 us
    psum x4 -> x0, waiting for transfers between devices: 216 us -> none  [advance_local(): class_sums = lax.psum(partial_sums, 'grp')]
    all_gather x0 -> x4, waiting for transfers between devices: none -> 74.4 us  [view_the_array(): return all_gather(slab_in, ax_name).sum(axis=0)]
    ppermute x8, waiting for transfers between devices: 15.9 us -> 33.9 us  [extended_2(): lax.ppermute(head, axis, [((i + 1) % count, i) for i in range(ends)])]
    reduce_sum x0 -> x4, other arithmetic: none -> 10.5 us  [view_the_array(): return all_gather(slab_in, ax_name).sum(axis=0)]
  transfers between devices with their start and end apart: 24 -> 24, of which waited for: 13 -> 22; matrix products, arithmetic and copies ran while one was open for 4% -> 2% of each run, Pallas kernels for 0% -> 0%
where the time goes in v1:
time: 886 us; the launch traced here: 877 us
  blocking collectives  381 us (43%)
  waiting for transfers between devices  323 us (36%)
  matrix products  64.6 us (7%)
  other arithmetic  59.7 us (7%)
  starting transfers between devices  26.5 us (3%)
  between operations  15.2 us (2%)
    psum x4, waiting for transfers between devices, retreat(): weighted_sums, shared_sum = lax.psum((weighted_sums, shared_sum), 'grp')  211 us
    psum x4, blocking collectives, advance_local(): lax.psum((jnp.sum(weighted * potential, axis=(1, 2, 3)), jnp.sum(weighted...  162 us
    psum x4, blocking collectives, retreat(): lagrange_adj = lax.psum(jnp.sum(first_part, axis=(1, 2, 3)), 'slab')  157 us
    all_gather x4, waiting for transfers between devices, view_the_array(): return all_gather(slab_in, ax_name).sum(axis=0)  74.4 us
    psum x1, blocking collectives, on_device(): mobility_total = lax.psum(mobility_acc, ('slab', 'grp'))  62.4 us
    ppermute x8, waiting for transfers between devices, extended_2(): lax.ppermute(head, axis, [((i + 1) % count, i) for i in range(ends)])  33.9 us
    dot_general x4, matrix products, retreat(): jnp.einsum('pk,kxzy->pxzy', member, class_adj, precision=lax.Precision.HI...  21 us
  transfers between devices with their start and end apart: 24, of which 22 were waited for; matrix products, arithmetic and copies ran while one was open for 2% of the time, Pallas kernels for 0%

profile of v1, /device:TPU:0, one launch (start us, length us, event | category | flops | bytes accessed | tf_op | source)
XLA Modules:
  0.0 876.5 jit_solution(2647473602031020269)
XLA Ops:
  7.2 2.1 fusion.9
  10.7 3.5 collective-permute-start.1
  17.0 4.1 collective-permute-done
  21.1 1.7 select_maximum_fusion.14
  22.9 22.3 %all-gather.9.cloned.1.call-done = f32[32,4,32,256]{3,2,1,0:T(8,128)} async-done(((f32[4,4,32,256]{3,2,1,0:T(8,128)}), f32[32,4,32,256]{3,2,1,0:T(8,128)}) %all-gather.9.cloned.1.call-update) | async-done | bytes 4194320 | tf_op jit(solution)/shard_map/all_gather | solution.py:15
  45.2 2.6 reduce_sum.232
  47.8 2.7 reduce_sum.233
  51.2 4.0 fusion.146
  55.2 40.3 %all-reduce.11 = (f32[4]{0:T(128)S(1)}, f32[4]{0:T(128)S(1)}) all-reduce(f32[4]{0:T(128)S(1)} %get-tuple-element.19, f32[4]{0:T(128)S(1)} %get-tuple-element.18), channel_id=1, replica_groups=mesh['slab'=16,'grp'=8] {'slab'}, use_global_device_ids=true, to_apply=%region_3.4 | all-reduce | flops 8 | bytes 64 | tf_op jit(solution)/shard_map/psum | solution.py:68
  101.9 4.4 collective-permute-done.2
  106.3 1.7 select_maximum_fusion.12
  108.0 17.4 %all-gather.11.cloned.1.call-done = f32[32,4,32,256]{3,2,1,0:T(8,128)} async-done(((f32[4,4,32,256]{3,2,1,0:T(8,128)}), f32[32,4,32,256]{3,2,1,0:T(8,128)}) %all-gather.11.cloned.1.call-update) | async-done | bytes 4194320 | tf_op jit(solution)/shard_map/all_gather | solution.py:15
  125.4 2.6 reduce_sum.236
  128.0 2.7 reduce_sum.237
  131.4 4.0 fusion.147
  135.4 40.3 %all-reduce.10 = (f32[4]{0:T(128)S(1)}, f32[4]{0:T(128)S(1)}) all-reduce(f32[4]{0:T(128)S(1)} %get-tuple-element.17, f32[4]{0:T(128)S(1)} %get-tuple-element.16), channel_id=1, replica_groups=mesh['slab'=16,'grp'=8] {'slab'}, use_global_device_ids=true, to_apply=%region_9.10 | all-reduce | flops 8 | bytes 64 | tf_op jit(solution)/shard_map/psum | solution.py:68
  181.8 4.4 collective-permute-done.4
  186.1 1.7 select_maximum_fusion.10
  187.9 17.4 %all-gather.13.cloned.1.call-done = f32[32,4,32,256]{3,2,1,0:T(8,128)} async-done(((f32[4,4,32,256]{3,2,1,0:T(8,128)}), f32[32,4,32,256]{3,2,1,0:T(8,128)}) %all-gather.13.cloned.1.call-update) | async-done | bytes 4194320 | tf_op jit(solution)/shard_map/all_gather | solution.py:15
  205.3 2.6 reduce_sum.240
  207.9 2.7 reduce_sum.241
  211.3 4.5 fusion.148
  215.8 40.4 %all-reduce.9 = (f32[4]{0:T(128)S(1)}, f32[4]{0:T(128)S(1)}) all-reduce(f32[4]{0:T(128)} %get-tuple-element.15, f32[4]{0:T(128)S(1)} %get-tuple-element.14), channel_id=1, replica_groups=mesh['slab'=16,'grp'=8] {'slab'}, use_global_device_ids=true, to_apply=%region_15.16 | all-reduce | flops 8 | bytes 64 | tf_op jit(solution)/shard_map/psum | solution.py:68
  263.8 4.4 collective-permute-done.6
  268.1 1.7 select_maximum_fusion.8
  269.9 17.4 %all-gather.15.cloned.1.call-done = f32[32,4,32,256]{3,2,1,0:T(8,128)} async-done(((f32[4,4,32,256]{3,2,1,0:T(8,128)}), f32[32,4,32,256]{3,2,1,0:T(8,128)}) %all-gather.15.cloned.1.call-update) | async-done | bytes 4194320 | tf_op jit(solution)/shard_map/all_gather | solution.py:15
  287.2 2.6 reduce_sum.244
  289.9 2.7 reduce_sum.245
  293.2 5.2 fusion.149
  298.5 40.4 %all-reduce.8 = (f32[4]{0:T(128)S(1)}, f32[4]{0:T(128)S(1)}) all-reduce(f32[4]{0:T(128)} %get-tuple-element.13, f32[4]{0:T(128)S(1)} %get-tuple-element.12), channel_id=1, replica_groups=mesh['slab'=16,'grp'=8] {'slab'}, use_global_device_ids=true, to_apply=%region_21.22 | all-reduce | flops 8 | bytes 64 | tf_op jit(solution)/shard_map/psum | solution.py:68
  338.9 3.3 fusion.138
  342.3 35.7 %psum.155 = f32[4]{0:T(128)S(1)} all-reduce(f32[4]{0:T(128)S(1)} %get-tuple-element.54), channel_id=1, replica_groups=mesh['slab'=16,'grp'=8] {'slab'}, use_global_device_ids=true, to_apply=%region_25.26 | all-reduce | flops 4 | bytes 32 | tf_op jit(solution)/shard_map/psum | solution.py:97
  378.0 3.2 subtract_reduce_fusion.3
  381.1 2.5 convolution_bitcast_fusion.3
  383.6 2.0 fusion.99
  385.7 3.9 collective-permute-start.9
  392.8 3.7 collective-permute-done.8
  396.5 1.7 select_maximum_fusion.6
  398.2 52.7 %all-reduce.27.cloned.1.call-done = (f32[4,4,32,256]{3,0,2,1:T(4,128)}, f32[4,32,256]{2,1,0:T(8,128)}) async-done(((f32[4,4,32,256]{3,0,2,1:T(4,128)}, f32[4,32,256]{2,1,0:T(8,128)}), (f32[4,4,32,256]{3,0,2,1:T(4,128)}, f32[4,32,256]{2,1,0:T(8,128)})) %all-reduce.27.cloned.1.call-update) | async-done | bytes 655376 | tf_op jit(solution)/shard_map/psum | solution.py:127
  451.0 6.0 fusion.139
  457.0 40.4 %psum.158 = f32[4]{0:T(128)S(1)} all-reduce(f32[4]{0:T(128)} %get-tuple-element.105), channel_id=1, replica_groups=mesh['slab'=16,'grp'=8] {'slab'}, use_global_device_ids=true, to_apply=%region_30.31 | all-reduce | flops 4 | bytes 32 | tf_op jit(solution)/shard_map/psum | solution.py:97
  498.1 3.1 subtract_reduce_fusion.2
  501.1 2.5 convolution_bitcast_fusion.2
  503.7 2.1 fusion.96
  509.7 4.2 collective-permute-done.10
  513.9 1.7 select_maximum_fusion.4
  515.6 51.0 %all-reduce.25.cloned.1.call-done = (f32[4,4,32,256]{3,0,2,1:T(4,128)}, f32[4,32,256]{2,1,0:T(8,128)}) async-done(((f32[4,4,32,256]{3,0,2,1:T(4,128)}, f32[4,32,256]{2,1,0:T(8,128)}), (f32[4,4,32,256]{3,0,2,1:T(4,128)}, f32[4,32,256]{2,1,0:T(8,128)})) %all-reduce.25.cloned.1.call-update) | async-done | bytes 655376 | tf_op jit(solution)/shard_map/psum | solution.py:127
  566.7 5.9 fusion.140
  572.6 40.4 %psum.161 = f32[4]{0:T(128)S(1)} all-reduce(f32[4]{0:T(128)} %get-tuple-element.107), channel_id=1, replica_groups=mesh['slab'=16,'grp'=8] {'slab'}, use_global_device_ids=true, to_apply=%region_35.36 | all-reduce | flops 4 | bytes 32 | tf_op jit(solution)/shard_map/psum | solution.py:97
  613.7 3.1 subtract_reduce_fusion.1
  616.8 2.5 convolution_bitcast_fusion.1
  619.3 2.1 fusion.93
  625.2 4.4 collective-permute-done.12
  629.6 1.7 select_maximum_fusion.2
  631.3 51.1 %all-reduce.23.cloned.1.call-done = (f32[4,4,32,256]{3,0,2,1:T(4,128)}, f32[4,32,256]{2,1,0:T(8,128)}) async-done(((f32[4,4,32,256]{3,0,2,1:T(4,128)}, f32[4,32,256]{2,1,0:T(8,128)}), (f32[4,4,32,256]{3,0,2,1:T(4,128)}, f32[4,32,256]{2,1,0:T(8,128)})) %all-reduce.23.cloned.1.call-update) | async-done | bytes 655376 | tf_op jit(solution)/shard_map/psum | solution.py:127
  682.4 5.9 fusion.141
  688.3 40.6 %psum.164 = f32[4]{0:T(128)S(1)} all-reduce(f32[4]{0:T(128)} %get-tuple-element.109), channel_id=1, replica_groups=mesh['slab'=16,'grp'=8] {'slab'}, use_global_device_ids=true, to_apply=%region_40.41 | all-reduce | flops 4 | bytes 32 | tf_op jit(solution)/shard_map/psum | solution.py:97
  729.6 3.1 subtract_reduce_fusion
  732.7 2.5 convolution_bitcast_fusion
  735.5 2.1 fusion.90
  737.5 62.4 %psum.167 = f32[4,4]{1,0:T(4,128)S(1)} all-reduce(f32[4,4]{1,0:T(4,128)S(1)} %convolution_add_fusion), channel_id=1, replica_groups=mesh['slab'=16,'grp'=8] {'slab','grp'}, use_global_device_ids=true, to_apply=%region_44.45 | all-reduce | flops 16 | bytes 128 | tf_op jit(solution)/shard_map/psum | solution.py:168
  803.9 4.4 collective-permute-done.14
  808.9 56.5 %all-reduce.21.cloned.1.call-done = (f32[4,4,32,256]{3,0,2,1:T(4,128)}, f32[4,32,256]{2,1,0:T(8,128)}) async-done(((f32[4,4,32,256]{3,0,2,1:T(4,128)}, f32[4,32,256]{2,1,0:T(8,128)}), (f32[4,4,32,256]{3,0,2,1:T(4,128)}, f32[4,32,256]{2,1,0:T(8,128)})) %all-reduce.21.cloned.1.call-update) | async-done | bytes 655376 | tf_op jit(solution)/shard_map/psum | solution.py:127
  865.4 3.2 fusion.20
  (205 shorter events, 45.0 us)
Async XLA Ops:
  7.2 9.3 %copy-start = (f32[4,4]{1,0:T(4,128)S(1)}, f32[4,4]{1,0:T(4,128)}, u32[]{:S(2)}) copy-start(f32[4,4]{1,0:T(4,128)} %param.9) | copy-start | bytes 196
  7.2 38.0 %all-gather.9.cloned.1.call-start = ((), (), s32[]{:S(2)}) async-start(), calls=%async_computation | async-start | bytes 4718592 | tf_op jit(solution)/shard_map/all_gather | solution.py:15
  10.3 5.3 copy-start.44
  10.3 6.1 copy-start.45
  10.3 115.1 %all-gather.11.cloned.1.call-start = ((), (), s32[]{:S(2)}) async-start(), calls=%async_computation.1 | async-start | bytes 4718592 | tf_op jit(solution)/shard_map/all_gather | solution.py:15
  10.7 6.3 collective-permute-start.1
  14.3 6.9 collective-permute-start
  16.4 79.1 %copy-start.22 = (f32[4,32,256]{2,1,0:T(8,128)}, f32[4,32,256]{2,1,0:T(8,128)S(1)}, u32[]{:S(2)}) copy-start(f32[4,32,256]{2,1,0:T(8,128)S(1)} %convert_element_type.22) | copy-start | bytes 393220
  55.2 41.8 %copy-start.10 = (f32[4,4,32,256]{3,0,2,1:T(4,128)}, f32[4,4,32,256]{3,0,2,1:T(4,128)S(1)}, u32[]{:S(2)}) copy-start(f32[4,4,32,256]{3,0,2,1:T(4,128)S(1)} %get-tuple-element.62) | copy-start | bytes 1572868
  55.2 41.8 %copy-start.12 = (f32[4,4,32,256]{3,0,2,1:T(4,128)}, f32[4,4,32,256]{3,0,2,1:T(4,128)S(1)}, u32[]{:S(2)}) copy-start(f32[4,4,32,256]{3,0,2,1:T(4,128)S(1)} %get-tuple-element.101) | copy-start | bytes 1572868
  98.0 107.2 %all-gather.13.cloned.1.call-start = ((), (), s32[]{:S(2)}) async-start(), calls=%async_computation.2 | async-start | bytes 4718592 | tf_op jit(solution)/shard_map/all_gather | solution.py:15
  98.1 3.8 collective-permute-start.3
  99.4 6.9 collective-permute-start.2
  100.7 75.0 %copy-start.24 = (f32[4,32,256]{2,1,0:T(8,128)}, f32[4,32,256]{2,1,0:T(8,128)S(1)}, u32[]{:S(2)}) copy-start(f32[4,32,256]{2,1,0:T(8,128)S(1)} %convert_element_type.23) | copy-start | bytes 393220
  135.4 41.6 %copy-start.14 = (f32[4,4,32,256]{3,0,2,1:T(4,128)}, f32[4,4,32,256]{3,0,2,1:T(4,128)S(1)}, u32[]{:S(2)}) copy-start(f32[4,4,32,256]{3,0,2,1:T(4,128)S(1)} %get-tuple-element.61) | copy-start | bytes 1572868
  135.4 41.6 %copy-start.16 = (f32[4,4,32,256]{3,0,2,1:T(4,128)}, f32[4,4,32,256]{3,0,2,1:T(4,128)S(1)}, u32[]{:S(2)}) copy-start(f32[4,4,32,256]{3,0,2,1:T(4,128)S(1)} %get-tuple-element.102) | copy-start | bytes 1572868
  177.9 109.3 %all-gather.15.cloned.1.call-start = ((), (), s32[]{:S(2)}) async-start(), calls=%async_computation.3 | async-start | bytes 4718592 | tf_op jit(solution)/shard_map/all_gather | solution.py:15
  178.0 3.8 collective-permute-start.5
  179.3 6.9 collective-permute-start.4
  181.8 23.5 %copy-start.41 = (f32[4,1,32,256]{3,0,2,1:T(4,128)}, f32[4,1,32,256]{3,0,2,1:T(4,128)S(1)}, u32[]{:S(2)}) copy-start(f32[4,1,32,256]{3,0,2,1:T(4,128)S(1)} %collective-permute-done.5) | copy-start | bytes 393220
  186.1 19.1 %copy-start.43 = (f32[4,1,32,256]{3,0,2,1:T(4,128)}, f32[4,1,32,256]{3,0,2,1:T(4,128)S(1)}, u32[]{:S(2)}) copy-start(f32[4,1,32,256]{3,0,2,1:T(4,128)S(1)} %collective-permute-done.4) | copy-start | bytes 393220
  215.8 43.1 %copy-start.18 = (f32[4,4,32,256]{3,0,2,1:T(4,128)}, f32[4,4,32,256]{3,0,2,1:T(4,128)S(1)}, u32[]{:S(2)}) copy-start(f32[4,4,32,256]{3,0,2,1:T(4,128)S(1)} %get-tuple-element.60) | copy-start | bytes 1572868
  215.8 43.1 %copy-start.20 = (f32[4,4,32,256]{3,0,2,1:T(4,128)}, f32[4,4,32,256]{3,0,2,1:T(4,128)S(1)}, u32[]{:S(2)}) copy-start(f32[4,4,32,256]{3,0,2,1:T(4,128)S(1)} %get-tuple-element.103) | copy-start | bytes 1572868
  259.9 191.1 %all-reduce.27.cloned.1.call-start = ((), (), s32[]{:S(2)}) async-start(), calls=%async_computation.7 | async-start | bytes 1310720 | tf_op jit(solution)/shard_map/psum | solution.py:127
  259.9 3.8 collective-permute-start.7
  261.3 6.9 collective-permute-start.6
  263.8 23.5 %copy-start.40 = (f32[4,1,32,256]{3,0,2,1:T(4,128)}, f32[4,1,32,256]{3,0,2,1:T(4,128)S(1)}, u32[]{:S(2)}) copy-start(f32[4,1,32,256]{3,0,2,1:T(4,128)S(1)} %collective-permute-done.7) | copy-start | bytes 393220
  268.1 19.1 %copy-start.42 = (f32[4,1,32,256]{3,0,2,1:T(4,128)}, f32[4,1,32,256]{3,0,2,1:T(4,128)S(1)}, u32[]{:S(2)}) copy-start(f32[4,1,32,256]{3,0,2,1:T(4,128)S(1)} %collective-permute-done.6) | copy-start | bytes 393220
  292.5 5.9 copy-start.33
  293.2 45.7 %copy-start.26 = (f32[4,32,256]{2,1,0:T(8,128)S(1)}, f32[4,32,256]{2,1,0:T(8,128)}, u32[]{:S(2)}) copy-start(f32[4,32,256]{2,1,0:T(8,128)} %get-tuple-element.57) | copy-start | bytes 393220
  338.9 39.0 %copy-start.34 = (f32[4,32,256]{2,1,0:T(8,128)S(1)}, f32[4,32,256]{2,1,0:T(8,128)}, u32[]{:S(2)}) copy-start(f32[4,32,256]{2,1,0:T(8,128)} %get-tuple-element.85) | copy-start | bytes 393220
  381.1 9.8 %copy-start.21 = (f32[4,4,32,256]{3,0,2,1:T(4,128)S(1)}, f32[4,4,32,256]{3,0,2,1:T(4,128)}, u32[]{:S(2)}) copy-start(f32[4,4,32,256]{3,0,2,1:T(4,128)} %get-tuple-element.56) | copy-start | bytes 1572868
  385.7 7.1 collective-permute-start.9
  389.6 6.9 collective-permute-start.8
  391.9 174.8 %all-reduce.25.cloned.1.call-start = ((), (), s32[]{:S(2)}) async-start(), calls=%async_computation.6 | async-start | bytes 1310720 | tf_op jit(solution)/shard_map/psum | solution.py:127
  392.8 58.2 %copy-start.36 = (f32[4,1,32,256]{3,0,2,1:T(4,128)}, f32[4,1,32,256]{3,0,2,1:T(4,128)S(1)}, u32[]{:S(2)}) copy-start(f32[4,1,32,256]{3,0,2,1:T(4,128)S(1)} %collective-permute-done.9) | copy-start | bytes 393220
  396.5 54.4 %copy-start.38 = (f32[4,1,32,256]{3,0,2,1:T(4,128)}, f32[4,1,32,256]{3,0,2,1:T(4,128)S(1)}, u32[]{:S(2)}) copy-start(f32[4,1,32,256]{3,0,2,1:T(4,128)S(1)} %collective-permute-done.8) | copy-start | bytes 393220
  451.0 47.1 %copy-start.19 = (f32[4,4,32,256]{3,0,2,1:T(4,128)S(1)}, f32[4,4,32,256]{3,0,2,1:T(4,128)}, u32[]{:S(2)}) copy-start(f32[4,4,32,256]{3,0,2,1:T(4,128)} %copy-done.18) | copy-start | bytes 1572868
  451.0 47.1 %copy-start.51 = (f32[4]{0:T(128)S(1)}, f32[4]{0:T(128)}, u32[]{:S(2)}) copy-start(f32[4]{0:T(128)} %copy-done.50) | copy-start | bytes 52
  503.7 5.2 copy-start.59
  505.7 3.9 collective-permute-start.11
  507.1 6.9 collective-permute-start.10
  508.4 58.3 %copy-start.17 = (f32[4,4,32,256]{3,0,2,1:T(4,128)S(1)}, f32[4,4,32,256]{3,0,2,1:T(4,128)}, u32[]{:S(2)}) copy-start(f32[4,4,32,256]{3,0,2,1:T(4,128)} %copy-done.16) | copy-start | bytes 1572868
  508.4 174.0 %all-reduce.23.cloned.1.call-start = ((), (), s32[]{:S(2)}) async-start(), calls=%async_computation.5 | async-start | bytes 1310720 | tf_op jit(solution)/shard_map/psum | solution.py:127
  509.7 57.0 %copy-start.37 = (f32[4,1,32,256]{3,0,2,1:T(4,128)}, f32[4,1,32,256]{3,0,2,1:T(4,128)S(1)}, u32[]{:S(2)}) copy-start(f32[4,1,32,256]{3,0,2,1:T(4,128)S(1)} %collective-permute-done.11) | copy-start | bytes 393220
  513.9 52.7 %copy-start.39 = (f32[4,1,32,256]{3,0,2,1:T(4,128)}, f32[4,1,32,256]{3,0,2,1:T(4,128)S(1)}, u32[]{:S(2)}) copy-start(f32[4,1,32,256]{3,0,2,1:T(4,128)S(1)} %collective-permute-done.10) | copy-start | bytes 393220
  566.7 47.0 %copy-start.15 = (f32[4,4,32,256]{3,0,2,1:T(4,128)S(1)}, f32[4,4,32,256]{3,0,2,1:T(4,128)}, u32[]{:S(2)}) copy-start(f32[4,4,32,256]{3,0,2,1:T(4,128)} %copy-done.14) | copy-start | bytes 1572868
  566.7 47.0 %copy-start.25 = (f32[4,32,256]{2,1,0:T(8,128)S(1)}, f32[4,32,256]{2,1,0:T(8,128)}, u32[]{:S(2)}) copy-start(f32[4,32,256]{2,1,0:T(8,128)} %copy-done.24) | copy-start | bytes 393220
  566.7 47.0 %copy-start.49 = (f32[4]{0:T(128)S(1)}, f32[4]{0:T(128)}, u32[]{:S(2)}) copy-start(f32[4]{0:T(128)} %copy-done.48) | copy-start | bytes 52
  619.3 4.8 copy-start.58
  621.4 3.8 collective-permute-start.13
  622.7 6.9 collective-permute-start.12
  624.0 58.3 %copy-start.13 = (f32[4,4,32,256]{3,0,2,1:T(4,128)S(1)}, f32[4,4,32,256]{3,0,2,1:T(4,128)}, u32[]{:S(2)}) copy-start(f32[4,4,32,256]{3,0,2,1:T(4,128)} %copy-done.12) | copy-start | bytes 1572868
  624.0 58.3 %copy-start.31 = (f32[4,32,256]{2,1,0:T(8,128)S(1)}, f32[4,32,256]{2,1,0:T(8,128)}, u32[]{:S(2)}) copy-start(f32[4,32,256]{2,1,0:T(8,128)} %copy-done.30) | copy-start | bytes 393220
  624.0 58.3 %copy-start.35 = (f32[4,32,256]{2,1,0:T(8,128)S(1)}, f32[4,32,256]{2,1,0:T(8,128)}, u32[]{:S(2)}) copy-start(f32[4,32,256]{2,1,0:T(8,128)} %get-tuple-element.89) | copy-start | bytes 393220
  624.1 241.4 %all-reduce.21.cloned.1.call-start = ((), (), s32[]{:S(2)}) async-start(), calls=%async_computation.4 | async-start | bytes 1310720 | tf_op jit(solution)/shard_map/psum | solution.py:127
  682.4 47.2 %copy-start.11 = (f32[4,4,32,256]{3,0,2,1:T(4,128)S(1)}, f32[4,4,32,256]{3,0,2,1:T(4,128)}, u32[]{:S(2)}) copy-start(f32[4,4,32,256]{3,0,2,1:T(4,128)} %copy-done.10) | copy-start | bytes 1572868
  682.4 47.2 %copy-start.23 = (f32[4,32,256]{2,1,0:T(8,128)S(1)}, f32[4,32,256]{2,1,0:T(8,128)}, u32[]{:S(2)}) copy-start(f32[4,32,256]{2,1,0:T(8,128)} %copy-done.22) | copy-start | bytes 393220
  682.4 47.2 %copy-start.29 = (f32[4,32,256]{2,1,0:T(8,128)S(1)}, f32[4,32,256]{2,1,0:T(8,128)}, u32[]{:S(2)}) copy-start(f32[4,32,256]{2,1,0:T(8,128)} %get-tuple-element.79) | copy-start | bytes 393220
  682.4 47.2 %copy-start.47 = (f32[4]{0:T(128)S(1)}, f32[4]{0:T(128)}, u32[]{:S(2)}) copy-start(f32[4]{0:T(128)} %copy-done.46) | copy-start | bytes 52
  729.6 5.6 copy-start.60
  799.9 3.9 collective-permute-start.15
  801.2 7.0 collective-permute-start.14
  802.5 62.9 %copy-start.28 = (f32[4,32,256]{2,1,0:T(8,128)S(1)}, f32[4,32,256]{2,1,0:T(8,128)}, u32[]{:S(2)}) copy-start(f32[4,32,256]{2,1,0:T(8,128)} %copy-done.27) | copy-start | bytes 393220
  (21 other events, 51.3 us)
Sparse Core Ops, SparseCore 0:
  10.4 34.7 all-gather.8
  98.1 27.1 all-gather.10
  178.0 27.1 all-gather.12
  260.0 27.1 all-gather.14
  392.0 58.9 all-reduce.26
  508.5 58.0 all-reduce.24
  624.2 58.1 all-reduce.22
  802.7 62.6 all-reduce.20
